TPU v7x, 128 devices: a whole 4x4x4 slice. The times are simulated.
128 devices in a mesh: blk: 16 (over x_lo, z, core), rep: 8 (over x_hi, y).
Axes of the slice: x: 4 (x_hi: 2, x_lo: 2; x = x_hi * 2 + x_lo), y: 4, z: 4, core: 2. Of those that a mesh axis runs over, the one named last changes fastest.
Arguments:
- features: bfloat16 [32768, 512], P(('blk', 'rep')), may hold values from -6 to 6
- weight: bfloat16 [512, 512], replicated, may hold values from -0.25 to 0.25
- layer_bias: float32 [512], replicated, may hold values from -4 to 4
- tile_values: bfloat16 [16, 8, 32, 8, 128, 128], P('blk', 'rep'), may hold values from -0.21875 to 0.21875
- tile_target: int32 [16, 8, 32, 8], P('blk', 'rep'), may hold values from 0 to 15, as said below
- tile_counts: int32 [16, 8, 32], P('blk', 'rep'), may hold values from 1 to 8, as said below
- cotangent: bfloat16 [32768, 512], P(('blk', 'rep')), may hold values from -6 to 6
Outputs:
- output: bfloat16 [32768, 512], P(('blk', 'rep'))
- grad_features: bfloat16 [32768, 512], P(('blk', 'rep'))
- grad_weight: float32 [512, 512], replicated
- grad_bias: float32 [512], replicated
Inputs may be any that keep to these rules, and one draw needn't show every extreme that they name: `tile_target`: within one source row tile of one list the 8 targets are distinct row tiles of the destination block. `tile_counts`: slots at or past the count are empty; every device's list has a source row tile with all 8 slots used.
All inputs are finite; a program needn't handle non-finite values.
Results may differ from a plain program's by a relative error of at most 0.008.
Values may be sent and summed in bfloat16 or wider, within the bound.
No kernel may reach another device: no remote copies, remote signals or barrier semaphores. Data moves between devices by JAX's collectives and lax.ppermute only.
A program may use at most 128 MiB of HBM per device.

v0:
```python
import math
import jax
import jax.numpy as jnp
from jax import lax
from jax.sharding import PartitionSpec as P


def swish_parts(summed, layer_bias, cotangent):
    shifted = summed + layer_bias[None, :]
    logistic = jax.nn.sigmoid(shifted)
    output = (shifted * logistic).astype(jnp.bfloat16)
    derivative = logistic * (1.0 + shifted * (1.0 - logistic))
    grad_summed = (cotangent.astype(jnp.float32) * derivative).astype(jnp.bfloat16)
    return (output, grad_summed)


def body(features, weight, layer_bias, tile_values, tile_target, tile_counts, cotangent):
    local_rows, feature_width = features.shape
    values = tile_values[0, 0]
    targets = tile_target[0, 0]
    counts = tile_counts[0, 0]
    tile_size = values.shape[-1]
    groups, slot_total = targets.shape
    dest_tiles = lax.axis_size("rep") * local_rows // tile_size
    active = lax.broadcasted_iota(jnp.int32, (groups, slot_total), 1) < counts[:, None]
    masked = jnp.where(active[:, :, None, None], values, jnp.zeros((), values.dtype))
    projected = jnp.dot(features, weight, preferred_element_type=jnp.float32).astype(jnp.bfloat16)

    def apply_group(running, group_id, sources):
        products = jnp.einsum(
            "sij,jf->sif", masked[group_id], sources, preferred_element_type=jnp.float32
        )
        return running.at[targets[group_id]].add(products)

    empty = jnp.zeros((dest_tiles, tile_size, feature_width), jnp.float32)
    running = empty
    incoming = lax.all_gather(projected, "blk", axis=0, tiled=True)
    number = incoming.shape[0] // tile_size
    blocks = incoming.reshape(number, tile_size, feature_width)

    def fold_group_step(current, offset):
        return (apply_group(current, offset, blocks[offset]), None)

    running, unused = lax.scan(fold_group_step, running, jnp.arange(number, dtype=jnp.int32))
    partial_value = running
    partial_value = partial_value.reshape(dest_tiles * tile_size, feature_width)
    summed = lax.psum_scatter(partial_value, "rep", scatter_dimension=0, tiled=True)
    output, grad_summed = swish_parts(summed, layer_bias, cotangent)
    grad_block = lax.all_gather(grad_summed, "rep", axis=0, tiled=True)
    grad_tiles = grad_block.reshape(dest_tiles, tile_size, feature_width)

    def back_group(group_id):
        gathered = grad_tiles[targets[group_id]]
        return jnp.einsum(
            "sij,sif->jf", masked[group_id], gathered, preferred_element_type=jnp.float32
        )

    row_count = lax.axis_size("blk") * local_rows
    number = row_count // tile_size

    def source_group_step(current, offset):
        return (current, back_group(offset))

    unused, terms = lax.scan(
        source_group_step, jnp.zeros((), jnp.float32), jnp.arange(number, dtype=jnp.int32)
    )
    grad_rows = lax.psum_scatter(
        terms.reshape(row_count, feature_width), "blk", scatter_dimension=0, tiled=True
    )
    grad_projected = grad_rows.astype(jnp.bfloat16)
    grad_features = lax.dot_general(
        grad_projected, weight, (((1,), (1,)), ((), ())), preferred_element_type=jnp.float32
    ).astype(jnp.bfloat16)
    weight_part = lax.dot_general(
        features, grad_projected, (((0,), (0,)), ((), ())), preferred_element_type=jnp.float32
    )
    bias_part = jnp.sum(grad_summed.astype(jnp.float32), axis=0)
    weight_total, bias_total = lax.psum((weight_part, bias_part), ("blk", "rep"))
    node_total = local_rows * lax.axis_size("blk") * lax.axis_size("rep")
    norm_scale = 1.0 / math.sqrt(node_total)
    return (output, grad_features, weight_total * norm_scale, bias_total * norm_scale)


def solution(mesh):
    placed = (
        P(("blk", "rep"), None),
        P(),
        P(),
        P("blk", "rep", None, None, None, None),
        P("blk", "rep", None, None),
        P("blk", "rep", None),
        P(("blk", "rep"), None),
    )
    return jax.shard_map(
        body,
        mesh=mesh,
        in_specs=placed,
        out_specs=(P(("blk", "rep"), None), P(("blk", "rep"), None), P(), P()),
        check_vma=False,
    )
```

profile of v0, /device:TPU:1, one launch (start us, length us, event | category | flops | bytes accessed | tf_op | source)
XLA Modules:
  0.0 912.2 jit_solution(14258984917883684823)
XLA Ops:
  10.3 11.9 %copy.12 = bf16[1,1,32,8,128,128]{4,5,3,2,1,0:T(8,128)(2,1)} copy(bf16[1,1,32,8,128,128]{5,4,3,2,1,0:T(8,128)(2,1)} %param.14) | data formatting | bytes 16777216 | tf_op args[3]
  22.4 7.3 bitcast_select_fusion
  29.7 21.7 %all-gather.3.cloned.1.call-done = bf16[4096,512]{1,0:T(8,128)(2,1)} async-done(((bf16[256,512]{1,0:T(8,128)(2,1)}), bf16[4096,512]{1,0:T(8,128)(2,1)}) %all-gather.3.cloned.1.call-update) | async-done | bytes 4194320 | tf_op jit(solution)/shard_map/all_gather | solution.py:37
  51.4 2.5 broadcast_in_dim.26
  53.9 268.6 %while.20 = (s32[]{:T(128)}, f32[16,128,512]{2,1,0:T(8,128)}, s32[32]{0:T(128)S(1)}, s32[32,8]{1,0:T(8,128)S(1)}, bf16[32,8,128,128]{2,3,1,0:T(8,128)(2,1)}, /*i...) while((s32[]{:T(128)}, f32[16,128,512]{2,1,0:T(8,128)}, s32[32]{0:T(128)S(1)}, ...), condition=%wide.region_2.3_spmd, body=%wide.region_0.2_spmd.sunk | while | flops 134742048 | bytes 8783087 | solution.py:44
  57.9 4.4 scatter_fusion
  66.3 4.5 scatter_fusion
  74.8 4.4 scatter_fusion
  83.2 4.4 scatter_fusion
  91.6 4.4 scatter_fusion
  100.0 4.4 scatter_fusion
  108.3 4.5 scatter_fusion
  116.8 4.4 scatter_fusion
  125.1 4.4 scatter_fusion
  133.6 4.4 scatter_fusion
  142.0 4.4 scatter_fusion
  150.4 4.4 scatter_fusion
  158.8 4.4 scatter_fusion
  167.2 4.4 scatter_fusion
  175.5 4.4 scatter_fusion
  183.9 4.4 scatter_fusion
  192.3 4.4 scatter_fusion
  200.6 4.4 scatter_fusion
  209.0 4.4 scatter_fusion
  217.4 4.4 scatter_fusion
  225.8 4.5 scatter_fusion
  234.2 4.4 scatter_fusion
  242.6 4.4 scatter_fusion
  251.0 4.4 scatter_fusion
  259.5 4.4 scatter_fusion
  267.8 4.4 scatter_fusion
  276.2 4.4 scatter_fusion
  284.6 4.4 scatter_fusion
  292.9 4.4 scatter_fusion
  301.3 4.4 scatter_fusion
  309.7 4.4 scatter_fusion
  318.0 4.4 scatter_fusion
  322.5 83.0 %reduce-scatter.3.cloned.1.call-done = f32[256,512]{1,0:T(8,128)} async-done(((f32[2048,512]{1,0:T(8,128)}), f32[256,512]{1,0:T(8,128)}) %reduce-scatter.3.cloned.1.call-update) | async-done | bytes 524304 | tf_op jit(solution)/shard_map/reduce_scatter | solution.py:47
  407.7 54.4 %all-gather.5.cloned.1.call-done = bf16[2048,512]{1,0:T(8,128)(2,1)} async-done(((bf16[256,512]{1,0:T(8,128)(2,1)}), bf16[2048,512]{1,0:T(8,128)(2,1)}) %all-gather.5.cloned.1.call-update) | async-done | bytes 2097168 | tf_op jit(solution)/shard_map/all_gather | solution.py:49
  462.1 215.8 %while.21 = (s32[]{:T(128)}, f32[32,128,512]{2,1,0:T(8,128)}, s32[32]{0:T(128)S(1)}, bf16[32,8,128,128]{2,3,1,0:T(8,128)(2,1)}, s32[32,8]{1,0:T(8,128)S(1)}, /*i...) while((s32[]{:T(128)}, f32[32,128,512]{2,1,0:T(8,128)}, s32[32]{0:T(128)S(1)}, ...), condition=%wide.region_5.6_spmd, body=%wide.region_4.5_spmd.sunk | while | flops 134218784 | bytes 3674899 | solution.py:64
  464.7 2.2 gather_fusion
  471.4 2.2 gather_fusion
  478.1 2.2 gather_fusion
  484.9 2.2 gather_fusion
  678.0 69.7 %reduce-scatter.5.cloned.1.call-done = f32[256,512]{1,0:T(8,128)} async-done(((f32[4096,512]{1,0:T(8,128)}), f32[256,512]{1,0:T(8,128)}) %reduce-scatter.5.cloned.1.call-update) | async-done | bytes 524304 | tf_op jit(solution)/shard_map/reduce_scatter | solution.py:67
  747.7 2.3 convolution_bitcast_fusion.1
  750.0 67.9 %psum.15 = f32[512]{0:T(512)S(1)} all-reduce(f32[512]{0:T(512)S(1)} %get-tuple-element.104), channel_id=1, replica_groups=mesh['blk'=16,'rep'=8] {'blk','rep'}, use_global_device_ids=true, to_apply=%region_9.10 | all-reduce | flops 512 | bytes 4096 | tf_op jit(solution)/shard_map/psum | solution.py:78
  820.6 82.4 %all-reduce.2.cloned.1.call-done = f32[512,512]{0,1:T(8,128)} async-done(((f32[512,512]{0,1:T(8,128)}), f32[512,512]{0,1:T(8,128)}) %all-reduce.2.cloned.1.call-update) | async-done | bytes 1048592 | tf_op jit(solution)/shard_map/psum | solution.py:78
  (285 shorter events, 219.9 us)
Async XLA Ops:
  7.2 1.0 copy-start
  7.2 44.2 %all-gather.3.cloned.1.call-start = ((), (), s32[]{:S(2)}) async-start(), calls=%async_computation.2 | async-start | bytes 4456448 | tf_op jit(solution)/shard_map/all_gather | solution.py:37
  10.2 12.0 %copy-start.3 = (s32[1,1,32,8]{2,3,1,0:T(8,128)S(1)}, s32[1,1,32,8]{2,3,1,0:T(8,128)}, u32[]{:S(2)}) copy-start(s32[1,1,32,8]{2,3,1,0:T(8,128)} %param.15) | copy-start | bytes 3076
  10.2 12.1 %copy-start.5 = (s32[1,1,32]{2,1,0:T(1,128)S(1)}, s32[1,1,32]{2,1,0:T(1,128)}, u32[]{:S(2)}) copy-start(s32[1,1,32]{2,1,0:T(1,128)} %param.16) | copy-start | bytes 388
  10.2 395.3 %reduce-scatter.3.cloned.1.call-start = ((), (), s32[]{:S(2)}) async-start(), calls=%async_computation.3 | async-start | bytes 4718592 | tf_op jit(solution)/shard_map/reduce_scatter | solution.py:47
  322.4 83.0 %copy-start.2 = (bf16[256,512]{1,0:T(8,128)(2,1)S(1)}, bf16[256,512]{1,0:T(8,128)(2,1)}, u32[]{:S(2)}) copy-start(bf16[256,512]{1,0:T(8,128)(2,1)} %param.17) | copy-start | bytes 786436
  322.4 83.0 %copy-start.4 = (f32[512]{0:T(512)S(1)}, f32[512]{0:T(512)}, u32[]{:S(2)}) copy-start(f32[512]{0:T(512)} %param.13) | copy-start | bytes 6148
  322.5 139.6 %all-gather.5.cloned.1.call-start = ((), (), s32[]{:S(2)}) async-start(), calls=%async_computation.4 | async-start | bytes 2359296 | tf_op jit(solution)/shard_map/all_gather | solution.py:49
  407.6 340.1 %reduce-scatter.5.cloned.1.call-start = ((), (), s32[]{:S(2)}) async-start(), calls=%async_computation.5 | async-start | bytes 8912896 | tf_op jit(solution)/shard_map/reduce_scatter | solution.py:67
  677.9 69.8 %copy-start.1 = (bf16[256,512]{1,0:T(8,128)(2,1)S(1)}, bf16[256,512]{1,0:T(8,128)(2,1)}, u32[]{:S(2)}) copy-start(bf16[256,512]{1,0:T(8,128)(2,1)} %param.11) | copy-start | bytes 786436
  677.9 225.1 %all-reduce.2.cloned.1.call-start = ((), (), s32[]{:S(2)}) async-start(), calls=%async_computation.6 | async-start | bytes 2097152 | tf_op jit(solution)/shard_map/psum | solution.py:78
Sparse Core Ops, SparseCore 0:
  10.3 41.0 all-gather.2
  322.6 82.8 reduce-scatter.2
  408.7 53.3 all-gather.4
  678.1 69.5 reduce-scatter.4
  753.6 149.3 all-reduce.1
where the time goes:
time: 918 us; the launch traced here: 912 us
  waiting for transfers between devices  311 us (34%)
  other arithmetic  153 us (17%)
  loops' own time  126 us (14%)
  local copies, waits for them, and re-layouts  125 us (14%)
  matrix products  115 us (13%)
  blocking collectives  67.9 us (7%)
  between operations  13.8 us (2%)
    scatter-add x32, other arithmetic, apply_group(): return running.at[targets[group_id]].add(products)  141 us
    reduce_scatter x1, waiting for transfers between devices, body(): lax.psum_scatter(partial_value, 'rep', scatter_dimension=0, tiled=True)  83 us
    psum x1, waiting for transfers between devices, body(): lax.psum((weight_part, bias_part), ('blk', 'rep'))  82.4 us
    gather x32, local copies, waits for them, and re-layouts, back_group(): gathered = grad_tiles[targets[group_id]]  70.6 us
    reduce_scatter x1, waiting for transfers between devices, body(): lax.psum_scatter(terms.reshape(row_count, feature_width), 'blk', scatter_...  69.7 us
    psum x1, blocking collectives, body(): lax.psum((weight_part, bias_part), ('blk', 'rep'))  67.9 us
    dot_general x32, matrix products, back_group(): jnp.einsum('sij,sif->jf', masked[group_id], gathered, preferred_element_t...  63.1 us
    another operation x1, loops' own time, body(): lax.scan(source_group_step, jnp.zeros((), jnp.float32), jnp.arange(number...  63 us
  transfers between devices with their start and end apart: 5, of which 5 were waited for; matrix products, arithmetic and copies ran while one was open for 2% of the time, Pallas kernels for 0%

commit v1 on v0

--- a/solution.py
+++ b/solution.py
@@ -75,7 +75,7 @@
         features, grad_projected, (((0,), (0,)), ((), ())), preferred_element_type=jnp.float32
     )
     bias_part = jnp.sum(grad_summed.astype(jnp.float32), axis=0)
-    weight_total, bias_total = lax.psum((weight_part, bias_part), ("blk", "rep"))
+    weight_total, bias_total = lax.psum(lax.psum((weight_part, bias_part), "blk"), "rep")
     node_total = local_rows * lax.axis_size("blk") * lax.axis_size("rep")
     norm_scale = 1.0 / math.sqrt(node_total)
     return (output, grad_features, weight_total * norm_scale, bias_total * norm_scale)

time: 918 us -> 978 us (1.065)
  waiting for transfers between devices: 311 us -> 387 us
  blocking collectives: 67.9 us -> 48.7 us
    psum x1 -> x2, waiting for transfers between devices: 82.4 us -> 158 us  [the longest x1 122 us: body(): lax.psum((weight_part, bias_part), 'blk')]
    psum x1 -> x2, blocking collectives: 67.9 us -> 48.7 us  [the longest x1 27.8 us: body(): lax.psum((weight_part, bias_part), 'blk')]
  transfers between devices with their start and end apart: 5 -> 6, of which waited for: 5 -> 6; matrix products, arithmetic and copies ran while one was open for 2% -> 2% of each run, Pallas kernels for 0% -> 0%
where the time goes in v1:
time: 978 us; the launch traced here: 968 us
  waiting for transfers between devices  387 us (40%)
  other arithmetic  153 us (16%)
  loops' own time  126 us (13%)
  local copies, waits for them, and re-layouts  125 us (13%)
  matrix products  115 us (12%)
  blocking collectives  48.7 us (5%)
  between operations  14.2 us (1%)
    scatter-add x32, other arithmetic, apply_group(): return running.at[targets[group_id]].add(products)  141 us
    psum x1, waiting for transfers between devices, body(): lax.psum((weight_part, bias_part), 'blk')  122 us
    reduce_scatter x1, waiting for transfers between devices, body(): lax.psum_scatter(partial_value, 'rep', scatter_dimension=0, tiled=True)  83.2 us
    gather x32, local copies, waits for them, and re-layouts, back_group(): gathered = grad_tiles[targets[group_id]]  70.6 us
    reduce_scatter x1, waiting for transfers between devices, body(): lax.psum_scatter(terms.reshape(row_count, feature_width), 'blk', scatter_...  69.6 us
    dot_general x32, matrix products, back_group(): jnp.einsum('sij,sif->jf', masked[group_id], gathered, preferred_element_t...  63.2 us
    another operation x1, loops' own time, body(): lax.scan(source_group_step, jnp.zeros((), jnp.float32), jnp.arange(number...  63 us
    another operation x1, loops' own time, body(): lax.scan(fold_group_step, running, jnp.arange(number, dtype=jnp.int32))  62.5 us
  transfers between devices with their start and end apart: 6, of which 6 were waited for; matrix products, arithmetic and copies ran while one was open for 2% of the time, Pallas kernels for 0%

profile of v1, /device:TPU:1, one launch (start us, length us, event | category | flops | bytes accessed | tf_op | source)
XLA Modules:
  0.0 967.9 jit_solution(13110976630129434047)
XLA Ops:
  10.3 11.9 %copy.12 = bf16[1,1,32,8,128,128]{4,5,3,2,1,0:T(8,128)(2,1)} copy(bf16[1,1,32,8,128,128]{5,4,3,2,1,0:T(8,128)(2,1)} %param.14) | data formatting | bytes 16777216 | tf_op args[3]
  22.4 7.3 bitcast_select_fusion
  29.7 21.7 %all-gather.3.cloned.1.call-done = bf16[4096,512]{1,0:T(8,128)(2,1)} async-done(((bf16[256,512]{1,0:T(8,128)(2,1)}), bf16[4096,512]{1,0:T(8,128)(2,1)}) %all-gather.3.cloned.1.call-update) | async-done | bytes 4194320 | tf_op jit(solution)/shard_map/all_gather | solution.py:37
  51.4 2.5 broadcast_in_dim.26
  53.9 268.3 %while.20 = (s32[]{:T(128)}, f32[16,128,512]{2,1,0:T(8,128)}, s32[32]{0:T(128)S(1)}, s32[32,8]{1,0:T(8,128)S(1)}, bf16[32,8,128,128]{2,3,1,0:T(8,128)(2,1)}, /*i...) while((s32[]{:T(128)}, f32[16,128,512]{2,1,0:T(8,128)}, s32[32]{0:T(128)S(1)}, ...), condition=%wide.region_2.3_spmd, body=%wide.region_0.2_spmd.sunk | while | flops 134742048 | bytes 8783087 | solution.py:44
  57.9 4.4 scatter_fusion
  66.3 4.4 scatter_fusion
  74.7 4.4 scatter_fusion
  83.1 4.4 scatter_fusion
  91.5 4.4 scatter_fusion
  99.9 4.4 scatter_fusion
  108.2 4.4 scatter_fusion
  116.6 4.4 scatter_fusion
  125.0 4.5 scatter_fusion
  133.4 4.4 scatter_fusion
  141.8 4.4 scatter_fusion
  150.2 4.4 scatter_fusion
  158.6 4.4 scatter_fusion
  167.0 4.4 scatter_fusion
  175.4 4.4 scatter_fusion
  183.8 4.4 scatter_fusion
  192.1 4.4 scatter_fusion
  200.5 4.4 scatter_fusion
  208.9 4.4 scatter_fusion
  217.2 4.4 scatter_fusion
  225.6 4.4 scatter_fusion
  234.0 4.4 scatter_fusion
  242.4 4.4 scatter_fusion
  250.8 4.4 scatter_fusion
  259.2 4.4 scatter_fusion
  267.6 4.4 scatter_fusion
  275.9 4.4 scatter_fusion
  284.3 4.4 scatter_fusion
  292.6 4.4 scatter_fusion
  301.0 4.4 scatter_fusion
  309.4 4.4 scatter_fusion
  317.8 4.4 scatter_fusion
  322.3 83.2 %reduce-scatter.3.cloned.1.call-done = f32[256,512]{1,0:T(8,128)} async-done(((f32[2048,512]{1,0:T(8,128)}), f32[256,512]{1,0:T(8,128)}) %reduce-scatter.3.cloned.1.call-update) | async-done | bytes 524304 | tf_op jit(solution)/shard_map/reduce_scatter | solution.py:47
  407.7 54.4 %all-gather.5.cloned.1.call-done = bf16[2048,512]{1,0:T(8,128)(2,1)} async-done(((bf16[256,512]{1,0:T(8,128)(2,1)}), bf16[2048,512]{1,0:T(8,128)(2,1)}) %all-gather.5.cloned.1.call-update) | async-done | bytes 2097168 | tf_op jit(solution)/shard_map/all_gather | solution.py:49
  462.1 215.8 %while.21 = (s32[]{:T(128)}, f32[32,128,512]{2,1,0:T(8,128)}, s32[32]{0:T(128)S(1)}, bf16[32,8,128,128]{2,3,1,0:T(8,128)(2,1)}, s32[32,8]{1,0:T(8,128)S(1)}, /*i...) while((s32[]{:T(128)}, f32[32,128,512]{2,1,0:T(8,128)}, s32[32]{0:T(128)S(1)}, ...), condition=%wide.region_5.6_spmd, body=%wide.region_4.5_spmd.sunk | while | flops 134218784 | bytes 3674899 | solution.py:64
  464.6 2.2 gather_fusion
  478.1 2.2 gather_fusion
  678.0 69.6 %reduce-scatter.5.cloned.1.call-done = f32[256,512]{1,0:T(8,128)} async-done(((f32[4096,512]{1,0:T(8,128)}), f32[256,512]{1,0:T(8,128)}) %reduce-scatter.5.cloned.1.call-update) | async-done | bytes 524304 | tf_op jit(solution)/shard_map/reduce_scatter | solution.py:67
  747.6 2.4 convolution_bitcast_fusion.1
  750.1 122.2 %all-reduce.3.cloned.1.call-done = f32[512,512]{0,1:T(8,128)} async-done(((f32[512,512]{0,1:T(8,128)}), f32[512,512]{0,1:T(8,128)}) %all-reduce.3.cloned.1.call-update) | async-done | bytes 1048592 | tf_op jit(solution)/shard_map/psum | solution.py:78
  872.3 27.8 %psum.30 = f32[512]{0:T(512)S(1)} all-reduce(f32[512]{0:T(512)S(1)} %get-tuple-element.104), channel_id=1, replica_groups=mesh['blk'=16,'rep'=8] {'blk'}, use_global_device_ids=true, to_apply=%region_10.11 | all-reduce | flops 512 | bytes 4096 | tf_op jit(solution)/shard_map/psum | solution.py:78
  900.1 20.9 %psum.31 = f32[512]{0:T(512)S(1)} all-reduce(f32[512]{0:T(512)S(1)} %psum.30), channel_id=1, replica_groups=mesh['blk'=16,'rep'=8] {'rep'}, use_global_device_ids=true, to_apply=%region_11.12 | all-reduce | flops 512 | bytes 4096 | tf_op jit(solution)/shard_map/psum | solution.py:78
  922.6 35.9 %all-reduce.5.cloned.1.call-done = f32[512,512]{0,1:T(8,128)} async-done(((f32[512,512]{0,1:T(8,128)}), f32[512,512]{0,1:T(8,128)}) %all-reduce.5.cloned.1.call-update) | async-done | bytes 1048592 | tf_op jit(solution)/shard_map/psum | solution.py:78
  (291 shorter events, 223.4 us)
Async XLA Ops:
  7.2 1.0 copy-start
  7.2 44.2 %all-gather.3.cloned.1.call-start = ((), (), s32[]{:S(2)}) async-start(), calls=%async_computation.2 | async-start | bytes 4456448 | tf_op jit(solution)/shard_map/all_gather | solution.py:37
  10.2 12.0 %copy-start.4 = (s32[1,1,32,8]{2,3,1,0:T(8,128)S(1)}, s32[1,1,32,8]{2,3,1,0:T(8,128)}, u32[]{:S(2)}) copy-start(s32[1,1,32,8]{2,3,1,0:T(8,128)} %param.15) | copy-start | bytes 3076
  10.2 12.1 %copy-start.6 = (s32[1,1,32]{2,1,0:T(1,128)S(1)}, s32[1,1,32]{2,1,0:T(1,128)}, u32[]{:S(2)}) copy-start(s32[1,1,32]{2,1,0:T(1,128)} %param.16) | copy-start | bytes 388
  10.2 395.3 %reduce-scatter.3.cloned.1.call-start = ((), (), s32[]{:S(2)}) async-start(), calls=%async_computation.3 | async-start | bytes 4718592 | tf_op jit(solution)/shard_map/reduce_scatter | solution.py:47
  322.2 83.3 %copy-start.3 = (bf16[256,512]{1,0:T(8,128)(2,1)S(1)}, bf16[256,512]{1,0:T(8,128)(2,1)}, u32[]{:S(2)}) copy-start(bf16[256,512]{1,0:T(8,128)(2,1)} %param.17) | copy-start | bytes 786436
  322.2 83.3 %copy-start.5 = (f32[512]{0:T(512)S(1)}, f32[512]{0:T(512)}, u32[]{:S(2)}) copy-start(f32[512]{0:T(512)} %param.13) | copy-start | bytes 6148
  322.2 139.9 %all-gather.5.cloned.1.call-start = ((), (), s32[]{:S(2)}) async-start(), calls=%async_computation.4 | async-start | bytes 2359296 | tf_op jit(solution)/shard_map/all_gather | solution.py:49
  407.6 340.0 %reduce-scatter.5.cloned.1.call-start = ((), (), s32[]{:S(2)}) async-start(), calls=%async_computation.5 | async-start | bytes 8912896 | tf_op jit(solution)/shard_map/reduce_scatter | solution.py:67
  677.9 69.7 %copy-start.2 = (bf16[256,512]{1,0:T(8,128)(2,1)S(1)}, bf16[256,512]{1,0:T(8,128)(2,1)}, u32[]{:S(2)}) copy-start(bf16[256,512]{1,0:T(8,128)(2,1)} %param.11) | copy-start | bytes 786436
  677.9 194.3 %all-reduce.3.cloned.1.call-start = ((), (), s32[]{:S(2)}) async-start(), calls=%async_computation.6 | async-start | bytes 2097152 | tf_op jit(solution)/shard_map/psum | solution.py:78
  747.6 174.0 %copy-start.1 = (f32[256,512]{1,0:T(8,128)S(1)}, f32[256,512]{1,0:T(8,128)}, u32[]{:S(2)}) copy-start(f32[256,512]{1,0:T(8,128)} %reduce-scatter.5.cloned.1.call-done) | copy-start | bytes 1572868
  750.0 208.4 %all-reduce.5.cloned.1.call-start = ((), (), s32[]{:S(2)}) async-start(), calls=%async_computation.7 | async-start | bytes 2097152 | tf_op jit(solution)/shard_map/psum | solution.py:78
Sparse Core Ops, SparseCore 0:
  10.3 41.0 all-gather.2
  322.3 83.1 reduce-scatter.2
  408.7 53.3 all-gather.4
  678.1 69.4 reduce-scatter.4
  750.6 121.5 all-reduce.2
  874.6 83.7 all-reduce.4
